TPU v7x, 512 devices: a whole 4x8x8 slice. The times are simulated.
512 devices in a mesh: dp: 64 (over z_hi, x, y), tile: 8 (over z_lo, core).
Axes of the slice: x: 4, y: 8, z: 8 (z_hi: 2, z_lo: 4; z = z_hi * 4 + z_lo), core: 2. Of those that a mesh axis runs over, the one named last changes fastest.
Arguments:
- feats: bfloat16 [4096, 2048], P('dp'), may hold values from -11 to 11
- jitter: bfloat16 [4096, 2048], P('dp'), may hold values from -1.5 to 1.5
- mask_ids: int32 [4096, 2], P('dp'), may hold values from 0 to 31
- proj_weight: bfloat16 [2048, 4096], P('dp', 'tile'), may hold values from -0.125 to 0.125
Outputs:
- feats_grad: float32 [4096, 2048], P('dp', 'tile')
- diag_corr: float32 [4096], P('tile')
- cross_power: float32 [], replicated
All inputs are finite; a program needn't handle non-finite values.
Results may differ from a plain program's by a relative error of at most 0.02.
Values may be sent and summed in bfloat16 or wider, within the bound.
No kernel may reach another device: no remote copies, remote signals or barrier semaphores. Data moves between devices by JAX's collectives and lax.ppermute only.
A program may use at most 64 MiB of HBM per device.

v0:
```python
import jax
import jax.numpy as jnp
from jax import lax
from jax.sharding import PartitionSpec as P

EMB = 4096
GROUPS = 32
LAMBDA_OFF = 0.0051
NORM_EPS = 1e-05
LOSS_SCALE = 65536.0


def masked_views(feats, jitter, mask_ids):
    width = feats.shape[1]
    group_size = width // GROUPS
    channel_group = lax.broadcasted_iota(jnp.int32, (1, width), 1) // group_size
    keep_a = (channel_group != mask_ids[:, 0:1]).astype(jnp.float32)
    keep_b = (channel_group != mask_ids[:, 1:2]).astype(jnp.float32)
    values = feats.astype(jnp.float32)
    view_a = (values * keep_a).astype(jnp.bfloat16)
    view_b = (values * keep_b + jitter.astype(jnp.float32)).astype(jnp.bfloat16)
    return (view_a, view_b, keep_a, keep_b)


def contract_last(left, right):
    return lax.dot_general(
        left, right, (((1,), (1,)), ((), ())), preferred_element_type=jnp.float32
    )


def on_device(feats, jitter, mask_ids, proj_weight):
    view_a, view_b, keep_a, keep_b = masked_views(feats, jitter, mask_ids)
    rows = feats.shape[0]
    total = rows * lax.axis_size("dp")
    piece = lax.all_gather(proj_weight, "dp", axis=0, tiled=True)
    raw_a = jnp.dot(view_a, piece, preferred_element_type=jnp.float32)
    raw_b = jnp.dot(view_b, piece, preferred_element_type=jnp.float32)
    raw_a = raw_a.astype(jnp.bfloat16)
    raw_b = raw_b.astype(jnp.bfloat16)
    values_a = raw_a.astype(jnp.float32)
    values_b = raw_b.astype(jnp.float32)
    moment_sums = lax.psum(
        (
            jnp.sum(values_a, axis=0),
            jnp.sum(values_a * values_a, axis=0),
            jnp.sum(values_b, axis=0),
            jnp.sum(values_b * values_b, axis=0),
        ),
        "dp",
    )
    mean_a = moment_sums[0] / total
    mean_b = moment_sums[2] / total
    inv_a = lax.rsqrt(moment_sums[1] / total - mean_a * mean_a + NORM_EPS)
    inv_b = lax.rsqrt(moment_sums[3] / total - mean_b * mean_b + NORM_EPS)
    norm_a = ((values_a - mean_a) * inv_a).astype(jnp.bfloat16)
    norm_b = ((values_b - mean_b) * inv_b).astype(jnp.bfloat16)
    outgoing_a, outgoing_b = (norm_a, norm_b)
    gathered_a, gathered_b = (
        lax.all_gather(outgoing_a, "dp", axis=0, tiled=True),
        lax.all_gather(outgoing_b, "dp", axis=0, tiled=True),
    )
    whole_a, whole_b = (gathered_a, gathered_b)
    za = norm_a.astype(jnp.float32)
    zb = norm_b.astype(jnp.float32)
    diag_corr = jnp.sum(whole_a.astype(jnp.float32) * whole_b.astype(jnp.float32), axis=0) / total
    gram_a, gram_b = (
        lax.psum(contract_last(norm_a, whole_a).astype(jnp.bfloat16), "tile").astype(jnp.float32),
        lax.psum(contract_last(norm_b, whole_b).astype(jnp.bfloat16), "tile").astype(jnp.float32),
    )
    trace_part = jnp.sum(gram_a * gram_b)
    gram_bf_a = gram_a.astype(jnp.bfloat16)
    gram_bf_b = gram_b.astype(jnp.bfloat16)
    coeff = -2.0 * (1.0 - diag_corr) - 2.0 * LAMBDA_OFF * diag_corr
    factor = 2.0 * LAMBDA_OFF / (total * total)
    grad_na = zb * coeff / total + factor * jnp.dot(
        gram_bf_b, whole_a, preferred_element_type=jnp.float32
    )
    grad_nb = za * coeff / total + factor * jnp.dot(
        gram_bf_a, whole_b, preferred_element_type=jnp.float32
    )
    sums = lax.psum(
        (
            jnp.sum(grad_na, axis=0),
            jnp.sum(grad_na * za, axis=0),
            jnp.sum(grad_nb, axis=0),
            jnp.sum(grad_nb * zb, axis=0),
            trace_part,
        ),
        "dp",
    )
    dz_a = (inv_a * (grad_na - sums[0] / total - za * (sums[1] / total))).astype(jnp.bfloat16)
    dz_b = (inv_b * (grad_nb - sums[2] / total - zb * (sums[3] / total))).astype(jnp.bfloat16)
    cross_power = sums[4] / (total * total) / EMB
    piece = lax.all_gather(proj_weight, "dp", axis=0, tiled=True)
    combined = keep_a * contract_last(dz_a, piece) + keep_b * contract_last(dz_b, piece)
    feats_grad = LOSS_SCALE * lax.psum_scatter(
        combined.astype(jnp.bfloat16), "tile", scatter_dimension=1, tiled=True
    ).astype(jnp.float32)
    return (feats_grad, diag_corr, cross_power)


def solution(mesh):
    in_specs = (P("dp", None), P("dp", None), P("dp", None), P("dp", "tile"))
    out_specs = (P("dp", "tile"), P("tile"), P())
    return jax.shard_map(
        on_device, mesh=mesh, in_specs=in_specs, out_specs=out_specs, check_vma=False
    )
```

profile of v0, /device:TPU:2, one launch (start us, length us, event | category | flops | bytes accessed | tf_op | source)
XLA Modules:
  0.0 1044.2 jit_solution(3339325027411994053)
XLA Ops:
  7.2 0.0 all-gather.4.cloned.1.call-start
  7.2 0.7 all-gather.4.cloned.1.call-update
  7.9 0.0 all-gather.6.cloned.1.call-start
  8.0 0.8 slice_bitcast_fusion
  8.7 147.5 %all-gather.4.cloned.1.call-done = bf16[2048,512]{1,0:T(8,128)(2,1)} async-done(((bf16[32,512]{1,0:T(8,128)(2,1)}), bf16[2048,512]{1,0:T(8,128)(2,1)}) %all-gather.4.cloned.1.call-update) | async-done | bytes 2097168 | tf_op jit(solution)/shard_map/all_gather | solution.py:35
  156.2 2.2 multiply_reduce_fusion.3
  158.5 2.3 fusion.42
  160.8 186.2 %all-reduce.1 = (f32[512]{0:T(512)S(1)}, f32[512]{0:T(512)S(1)}, f32[512]{0:T(512)S(1)}, f32[512]{0:T(512)S(1)}) all-reduce(f32[512]{0:T(512)S(1)} %get-tuple-element.10, f32[512]{0:T(512)S(1)} %get-tuple-element.9, f32[512]{0:T(512)S(1)} %get-tuple-element.8, f32[512]{0:T(512)S(1)} %get-tuple-element.7), channel_id=1, replica_groups=mesh['dp'=64,'tile'=8] {'dp'}, use_global_device_ids=true, to_apply=%region_3.4 | all-reduce | flops 2048 | bytes 16384 | tf_op jit(solution)/shard_map/psum | solution.py:42
  347.0 0.6 multiply_convert_fusion
  347.6 0.0 all-gather.6.cloned.1.call-update
  347.6 0.0 all-gather.8.cloned.1.call-start
  347.7 0.6 multiply_convert_fusion.1
  348.3 0.0 copy-start.3
  348.3 0.0 all-gather.8.cloned.1.call-update
  348.4 0.0 all-reduce.5.cloned.1.call-start
  348.4 186.0 %all-gather.6.cloned.1.call-done = bf16[4096,512]{1,0:T(8,128)(2,1)} async-done(((bf16[64,512]{1,0:T(8,128)(2,1)}), bf16[4096,512]{1,0:T(8,128)(2,1)}) %all-gather.6.cloned.1.call-update) | async-done | bytes 4194320 | tf_op jit(solution)/shard_map/all_gather | solution.py:59
  534.4 4.4 convolution_convert_fusion
  538.8 152.4 %all-gather.8.cloned.1.call-done = bf16[4096,512]{1,0:T(8,128)(2,1)} async-done(((bf16[64,512]{1,0:T(8,128)(2,1)}), bf16[4096,512]{1,0:T(8,128)(2,1)}) %all-gather.8.cloned.1.call-update) | async-done | bytes 4194320 | tf_op jit(solution)/shard_map/all_gather | solution.py:60
  691.2 0.0 copy-done.3
  691.2 4.4 convolution_convert_fusion.1
  695.6 0.0 all-reduce.5.cloned.1.call-update
  695.6 0.0 copy-start.2
  695.6 0.0 reduce-scatter.2.cloned.1.call-start
  695.6 4.6 multiply_reduce_fusion
  700.3 0.6 multiply_subtract_fusion
  700.8 68.8 %all-reduce.5.cloned.1.call-done = (bf16[64,4096]{1,0:T(8,128)(2,1)}, bf16[64,4096]{1,0:T(8,128)(2,1)}) async-done(((bf16[64,4096]{1,0:T(8,128)(2,1)}, bf16[64,4096]{1,0:T(8,128)(2,1)}), (bf16[64,4096]{1,0:T(8,128)(2,1)}, bf16[64,4096]{1,0:T(8,128)(2,1)})) %all-reduce.5.cloned.1.call-update) | async-done | bytes 1048592 | tf_op jit(solution)/shard_map/psum | solution.py:68
  769.7 0.0 copy-start
  769.7 0.0 copy-start.4
  769.7 2.2 multiply_reduce_fusion.1
  771.9 0.0 copy-done.2
  771.9 0.0 copy-start.1
  771.9 3.4 fusion.40
  775.3 0.0 copy-done
  775.3 0.0 copy-done.4
  775.3 0.9 fusion.41
  776.2 196.4 %all-reduce = (f32[512]{0:T(512)S(1)}, f32[512]{0:T(512)S(1)}, f32[512]{0:T(512)S(1)}, f32[512]{0:T(512)S(1)}, f32[]{:T(128)}) all-reduce(f32[512]{0:T(512)S(1)} %get-tuple-element.6, f32[512]{0:T(512)S(1)} %get-tuple-element.5, f32[512]{0:T(512)S(1)} %get-tuple-element.4, ...), channel_id=1, replica_groups=mesh['dp'=64,'tile'=8] {'dp'}, use_global_device_ids=true, to_apply=%region_13.14 | all-reduce | flops 2049 | bytes 16392 | tf_op jit(solution)/shard_map/psum | solution.py:81
  972.6 0.0 copy-done.1
  972.6 0.8 convolution_select_fusion.1
  973.3 1.5 fusion.1
  974.8 0.0 reduce-scatter.2.cloned.1.call-update
  975.4 59.7 %reduce-scatter.2.cloned.1.call-done = bf16[64,256]{1,0:T(8,128)(2,1)} async-done(((bf16[64,2048]{1,0:T(8,128)(2,1)}), bf16[64,256]{1,0:T(8,128)(2,1)}) %reduce-scatter.2.cloned.1.call-update) | async-done | bytes 32784 | tf_op jit(solution)/shard_map/reduce_scatter | solution.py:96
  1035.1 1.4 convert_multiply_fusion.6
  (5 shorter events, 0.0 us)
Async XLA Ops:
  7.2 149.1 %all-gather.4.cloned.1.call-start = ((), (), s32[]{:S(2)}) async-start(), calls=%async_computation.1 | async-start | bytes 2129920 | tf_op jit(solution)/shard_map/all_gather | solution.py:35
  7.9 526.5 %all-gather.6.cloned.1.call-start = ((), (), s32[]{:S(2)}) async-start(), calls=%async_computation.2 | async-start | bytes 4259840 | tf_op jit(solution)/shard_map/all_gather | solution.py:59
  347.6 343.6 %all-gather.8.cloned.1.call-start = ((), (), s32[]{:S(2)}) async-start(), calls=%async_computation.3 | async-start | bytes 4259840 | tf_op jit(solution)/shard_map/all_gather | solution.py:60
  348.3 342.9 %copy-start.3 = (bf16[64,512]{1,0:T(8,128)(2,1)S(1)}, bf16[64,512]{1,0:T(8,128)(2,1)}, u32[]{:S(2)}) copy-start(bf16[64,512]{1,0:T(8,128)(2,1)} %multiply_convert_fusion.1) | copy-start | bytes 196612
  348.4 421.3 %all-reduce.5.cloned.1.call-start = ((), (), s32[]{:S(2)}) async-start(), calls=%async_computation.5 | async-start | bytes 2097152 | tf_op jit(solution)/shard_map/psum | solution.py:68
  695.6 76.3 %copy-start.2 = (bf16[64,512]{1,0:T(8,128)(2,1)S(1)}, bf16[64,512]{1,0:T(8,128)(2,1)}, u32[]{:S(2)}) copy-start(bf16[64,512]{1,0:T(8,128)(2,1)} %multiply_convert_fusion) | copy-start | bytes 196612
  695.6 339.5 %reduce-scatter.2.cloned.1.call-start = ((), (), s32[]{:S(2)}) async-start(), calls=%async_computation.4 | async-start | bytes 294912 | tf_op jit(solution)/shard_map/reduce_scatter | solution.py:96
  769.7 5.6 copy-start
  769.7 5.6 copy-start.4
  771.9 200.6 %copy-start.1 = (bf16[2048,512]{1,0:T(8,128)(2,1)S(1)}, bf16[2048,512]{1,0:T(8,128)(2,1)}, u32[]{:S(2)}) copy-start(bf16[2048,512]{1,0:T(8,128)(2,1)} %all-gather.4.cloned.1.call-done) | copy-start | bytes 6291460
Sparse Core Ops, SparseCore 0:
  12.5 143.6 all-gather.3
  347.7 186.5 all-gather.5
  538.9 152.2 all-gather.7
  695.7 73.9 all-reduce.4
  974.9 60.1 reduce-scatter.1
where the time goes:
time: 1040 us
  waiting for transfers between devices  615 us (59%)
  blocking collectives  383 us (37%)
  matrix products  19.7 us (2%)
  between operations  15.6 us (2%)
    psum x1, blocking collectives, on_device(): lax.psum((jnp.sum(grad_na, axis=0), jnp.sum(grad_na * za, axis=0), jnp.su...  196 us
    psum x1, blocking collectives, on_device(): lax.psum((jnp.sum(values_a, axis=0), jnp.sum(values_a * values_a, axis=0)...  186 us
    all_gather x1, waiting for transfers between devices, on_device(): lax.all_gather(outgoing_a, 'dp', axis=0, tiled=True)  186 us
    all_gather x1, waiting for transfers between devices, on_device(): lax.all_gather(outgoing_b, 'dp', axis=0, tiled=True)  152 us
    all_gather x1, waiting for transfers between devices, on_device(): piece = lax.all_gather(proj_weight, 'dp', axis=0, tiled=True)  148 us
    psum x1, waiting for transfers between devices, on_device(): lax.psum(contract_last(norm_b, whole_b).astype(jnp.bfloat16), 'tile')  68.8 us
    reduce_scatter x1, waiting for transfers between devices, on_device(): lax.psum_scatter(combined.astype(jnp.bfloat16), 'tile', scatter_dimension...  59.7 us
  transfers between devices with their start and end apart: 5, of which 5 were waited for; matrix products, arithmetic and copies ran while one was open for 1% of the time, Pallas kernels for 0%

commit v1 on v0

--- a/solution.py
+++ b/solution.py
@@ -56,7 +56,9 @@
     norm_b = ((values_b - mean_b) * inv_b).astype(jnp.bfloat16)
     outgoing_a, outgoing_b = (norm_a, norm_b)
     gathered_a, gathered_b = (
-        lax.all_gather(outgoing_a, "dp", axis=0, tiled=True),
+        jnp.concatenate(
+            lax.all_to_all(jnp.stack([outgoing_a] * lax.axis_size("dp")), "dp", 0, 0), axis=0
+        ),
         lax.all_gather(outgoing_b, "dp", axis=0, tiled=True),
     )
     whole_a, whole_b = (gathered_a, gathered_b)

time: 1040 us -> 950 us (0.913)
  the two profiles are of different devices: /device:TPU:2 before, /device:TPU:4 now
where the time goes in v1:
time: 950 us; the launch traced here: 949 us
  waiting for transfers between devices  498 us (52%)
  blocking collectives  323 us (34%)
  starting transfers between devices  80.3 us (8%)
  matrix products  19.7 us (2%)
  between operations  15.6 us (2%)
  other arithmetic  9.51 us (1%)
    psum x1, blocking collectives, on_device(): lax.psum((jnp.sum(grad_na, axis=0), jnp.sum(grad_na * za, axis=0), jnp.su...  165 us
    psum x1, blocking collectives, on_device(): lax.psum((jnp.sum(values_a, axis=0), jnp.sum(values_a * values_a, axis=0)...  158 us
    all_gather x1, waiting for transfers between devices, on_device(): piece = lax.all_gather(proj_weight, 'dp', axis=0, tiled=True)  148 us
    all_gather x1, waiting for transfers between devices, on_device(): lax.all_gather(outgoing_b, 'dp', axis=0, tiled=True)  128 us
    reduce_scatter x1, waiting for transfers between devices, on_device(): lax.psum_scatter(combined.astype(jnp.bfloat16), 'tile', scatter_dimension...  91 us
    all_to_all x1, starting transfers between devices, on_device(): lax.all_to_all(jnp.stack([outgoing_a] * lax.axis_size('dp')), 'dp', 0, 0)  80.2 us
    psum x1, waiting for transfers between devices, on_device(): lax.psum(contract_last(norm_b, whole_b).astype(jnp.bfloat16), 'tile')  68.8 us
    all_to_all x1, waiting for transfers between devices, on_device(): lax.all_to_all(jnp.stack([outgoing_a] * lax.axis_size('dp')), 'dp', 0, 0)  61.5 us
  transfers between devices with their start and end apart: 5, of which 5 were waited for; matrix products, arithmetic and copies ran while one was open for 1% of the time, Pallas kernels for 0%

profile of v1, /device:TPU:4, one launch (start us, length us, event | category | flops | bytes accessed | tf_op | source)
XLA Modules:
  0.0 949.3 jit_solution(12050009236728042560)
XLA Ops:
  7.2 0.0 all-gather.3.cloned.1.call-start
  7.2 0.7 all-gather.3.cloned.1.call-update
  7.9 0.8 slice_bitcast_fusion
  8.7 147.6 %all-gather.3.cloned.1.call-done = bf16[2048,512]{1,0:T(8,128)(2,1)} async-done(((bf16[32,512]{1,0:T(8,128)(2,1)}), bf16[2048,512]{1,0:T(8,128)(2,1)}) %all-gather.3.cloned.1.call-update) | async-done | bytes 2097168 | tf_op jit(solution)/shard_map/all_gather | solution.py:35
  156.3 2.2 multiply_reduce_fusion.3
  158.5 2.3 fusion.42
  160.8 157.7 %all-reduce.1 = (f32[512]{0:T(512)S(1)}, f32[512]{0:T(512)S(1)}, f32[512]{0:T(512)S(1)}, f32[512]{0:T(512)S(1)}) all-reduce(f32[512]{0:T(512)S(1)} %get-tuple-element.10, f32[512]{0:T(512)S(1)} %get-tuple-element.9, f32[512]{0:T(512)S(1)} %get-tuple-element.8, f32[512]{0:T(512)S(1)} %get-tuple-element.7), channel_id=1, replica_groups=mesh['dp'=64,'tile'=8] {'dp'}, use_global_device_ids=true, to_apply=%region_3.4 | all-reduce | flops 2048 | bytes 16384 | tf_op jit(solution)/shard_map/psum | solution.py:42
  318.6 2.5 stack.2
  321.0 80.2 %all-to-all-start = ((bf16[64,64,512]{2,1,0:T(8,128)(2,1)}), bf16[64,64,512]{2,1,0:T(8,128)(2,1)}, u32[]{:S(2)}, u32[]{:S(2)}) async-start(bf16[64,64,512]{2,1,0:T(8,128)(2,1)} %stack.2), calls=%async_computation | async-start | bytes 8388608 | tf_op jit(solution)/shard_map/all_to_all | solution.py:60
  401.2 0.0 all-gather.5.cloned.1.call-start
  401.3 0.6 multiply_convert_fusion.1
  401.9 0.0 copy-start.2
  401.9 0.0 all-gather.5.cloned.1.call-update
  402.0 0.0 all-reduce.5.cloned.1.call-start
  402.0 61.5 %all-to-all-done = bf16[64,64,512]{2,1,0:T(8,128)(2,1)} async-done(((bf16[64,64,512]{2,1,0:T(8,128)(2,1)}), bf16[64,64,512]{2,1,0:T(8,128)(2,1)}, u32[]{:S(2)}, u32[]{:S(2)}) %all-to-all-start) | async-done | bytes 4194336 | tf_op jit(solution)/shard_map/all_to_all | solution.py:60
  463.5 4.4 convolution_convert_fusion
  467.8 128.5 %all-gather.5.cloned.1.call-done = bf16[4096,512]{1,0:T(8,128)(2,1)} async-done(((bf16[64,512]{1,0:T(8,128)(2,1)}), bf16[4096,512]{1,0:T(8,128)(2,1)}) %all-gather.5.cloned.1.call-update) | async-done | bytes 4194320 | tf_op jit(solution)/shard_map/all_gather | solution.py:62
  596.3 0.0 copy-done.2
  596.3 4.4 convolution_convert_fusion.1
  600.7 0.0 all-reduce.5.cloned.1.call-update
  600.7 0.0 reduce-scatter.2.cloned.1.call-start
  600.7 4.6 multiply_reduce_fusion
  605.3 0.6 multiply_subtract_fusion
  605.9 68.8 %all-reduce.5.cloned.1.call-done = (bf16[64,4096]{1,0:T(8,128)(2,1)}, bf16[64,4096]{1,0:T(8,128)(2,1)}) async-done(((bf16[64,4096]{1,0:T(8,128)(2,1)}, bf16[64,4096]{1,0:T(8,128)(2,1)}), (bf16[64,4096]{1,0:T(8,128)(2,1)}, bf16[64,4096]{1,0:T(8,128)(2,1)})) %all-reduce.5.cloned.1.call-update) | async-done | bytes 1048592 | tf_op jit(solution)/shard_map/psum | solution.py:70
  674.7 0.0 copy-start
  674.7 0.0 copy-start.3
  674.7 2.2 multiply_reduce_fusion.1
  677.0 0.0 copy-start.1
  677.0 3.4 fusion.41
  680.3 0.0 copy-done
  680.3 0.0 copy-done.3
  680.4 0.9 fusion.40
  681.2 165.1 %all-reduce = (f32[512]{0:T(512)S(1)}, f32[512]{0:T(512)S(1)}, f32[512]{0:T(512)S(1)}, f32[512]{0:T(512)S(1)}, f32[]{:T(128)}) all-reduce(f32[512]{0:T(512)S(1)} %get-tuple-element.6, f32[512]{0:T(512)S(1)} %get-tuple-element.5, f32[512]{0:T(512)S(1)} %get-tuple-element.4, ...), channel_id=1, replica_groups=mesh['dp'=64,'tile'=8] {'dp'}, use_global_device_ids=true, to_apply=%region_13.14 | all-reduce | flops 2049 | bytes 16392 | tf_op jit(solution)/shard_map/psum | solution.py:83
  846.3 0.0 copy-done.1
  846.3 0.8 convolution_select_fusion.1
  847.1 1.5 fusion.1
  848.5 0.0 reduce-scatter.2.cloned.1.call-update
  849.2 91.0 %reduce-scatter.2.cloned.1.call-done = bf16[64,256]{1,0:T(8,128)(2,1)} async-done(((bf16[64,2048]{1,0:T(8,128)(2,1)}), bf16[64,256]{1,0:T(8,128)(2,1)}) %reduce-scatter.2.cloned.1.call-update) | async-done | bytes 32784 | tf_op jit(solution)/shard_map/reduce_scatter | solution.py:98
  940.2 1.4 convert_multiply_fusion.6
  (7 shorter events, 0.0 us)
Async XLA Ops:
  7.2 149.1 %all-gather.3.cloned.1.call-start = ((), (), s32[]{:S(2)}) async-start(), calls=%async_computation.2 | async-start | bytes 2129920 | tf_op jit(solution)/shard_map/all_gather | solution.py:35
  321.0 142.4 %all-to-all-start = ((bf16[64,64,512]{2,1,0:T(8,128)(2,1)}), bf16[64,64,512]{2,1,0:T(8,128)(2,1)}, u32[]{:S(2)}, u32[]{:S(2)}) async-start(bf16[64,64,512]{2,1,0:T(8,128)(2,1)} %stack.2), calls=%async_computation | async-start | bytes 8388608 | tf_op jit(solution)/shard_map/all_to_all | solution.py:60
  401.2 195.1 %all-gather.5.cloned.1.call-start = ((), (), s32[]{:S(2)}) async-start(), calls=%async_computation.3 | async-start | bytes 4259840 | tf_op jit(solution)/shard_map/all_gather | solution.py:62
  401.9 194.4 %copy-start.2 = (bf16[64,512]{1,0:T(8,128)(2,1)S(1)}, bf16[64,512]{1,0:T(8,128)(2,1)}, u32[]{:S(2)}) copy-start(bf16[64,512]{1,0:T(8,128)(2,1)} %multiply_convert_fusion.1) | copy-start | bytes 196612
  402.0 272.8 %all-reduce.5.cloned.1.call-start = ((), (), s32[]{:S(2)}) async-start(), calls=%async_computation.5 | async-start | bytes 2097152 | tf_op jit(solution)/shard_map/psum | solution.py:70
  600.7 339.5 %reduce-scatter.2.cloned.1.call-start = ((), (), s32[]{:S(2)}) async-start(), calls=%async_computation.4 | async-start | bytes 294912 | tf_op jit(solution)/shard_map/reduce_scatter | solution.py:98
  674.7 5.6 copy-start
  674.7 5.6 copy-start.3
  677.0 169.3 %copy-start.1 = (bf16[2048,512]{1,0:T(8,128)(2,1)S(1)}, bf16[2048,512]{1,0:T(8,128)(2,1)}, u32[]{:S(2)}) copy-start(bf16[2048,512]{1,0:T(8,128)(2,1)} %all-gather.3.cloned.1.call-done) | copy-start | bytes 6291460
Sparse Core Ops, SparseCore 0:
  12.5 143.7 all-gather.2
  407.2 189.0 all-gather.4
  600.8 73.8 all-reduce.4
  848.7 91.4 reduce-scatter.1
